TPU v7x, 512 devices: a whole 4x4x16 slice. The times are simulated.
512 devices in a mesh: pipe: 16 (over x, y), expert: 32 (over z, core).
Axes of the slice: x: 4, y: 4, z: 16, core: 2. Of those that a mesh axis runs over, the one named last changes fastest.
Arguments:
- fwd_state: bfloat16 [16, 2048, 3584], P('pipe', 'expert'), may hold values from -6 to 6
- rev_state: bfloat16 [16, 2048, 3584], P('pipe', 'expert'), may hold values from -6 to 6
- norm_gain: float32 [16, 3584], P('pipe'), may hold values from 0.5 to 1.5
- w_gate: bfloat16 [16, 3584, 4096], P('pipe', None, 'expert'), may hold values from -0.09375 to 0.09375
- w_up: bfloat16 [16, 3584, 4096], P('pipe', None, 'expert'), may hold values from -0.09375 to 0.09375
- w_down: bfloat16 [16, 4096, 3584], P('pipe', 'expert'), may hold values from -0.1875 to 0.1875
- routes_fwd: int32 [3, 16, 2048, 8], P(None, 'pipe', 'expert'), may hold values from 0 to 255, as said below
- scores_fwd: float32 [3, 16, 2048, 8], P(None, 'pipe', 'expert'), may hold values from 0.02 to 1
- routes_rev: int32 [3, 16, 2048, 8], P(None, 'pipe', 'expert'), may hold values from 0 to 255, as said below
- scores_rev: float32 [3, 16, 2048, 8], P(None, 'pipe', 'expert'), may hold values from 0.02 to 1
Outputs:
- fwd_out: bfloat16 [16, 2048, 3584], P('pipe', 'expert')
- rev_out: bfloat16 [16, 2048, 3584], P('pipe', 'expert')
Inputs may be any that keep to these rules, and one draw needn't show every extreme that they name: `routes_fwd`: each row names 8 different experts, all from at most 4 of the 8 groups of 32 consecutive experts. Among the 64 rows of one device, each expert below 4 is named by 1 to 4 rows, and one of them by exactly 4. `routes_rev`: as for routes_fwd.
All inputs are finite; a program needn't handle non-finite values.
Results may differ from a plain program's by a relative error of at most 0.003.
Values may be sent and summed in bfloat16 or wider, within the bound.
No kernel may reach another device: no remote copies, remote signals or barrier semaphores. Data moves between devices by JAX's collectives and lax.ppermute only.
A program may use at most 64 MiB of HBM per device.

v0:
```python
import jax
import jax.numpy as jnp
from jax import lax
from jax.sharding import Mesh, PartitionSpec as P

CAP = 4
STEPS = 3
GROUP = 4
PAIRS = 2

EPSILON = 1e-06
ROUTE_SCALE = 2.5


def shifted(value, axis, steps):
    count = lax.axis_size(axis)
    pairs = [(source, (source + steps) % count) for source in range(count)]
    return lax.ppermute(value, axis, pairs)


def after(value, *earlier):
    return lax.optimization_barrier((value, *earlier))[0]


def exact_pick(table, rows):
    return jnp.dot(table.astype(jnp.bfloat16), rows, preferred_element_type=jnp.float32)


def route_tables(route_ids, route_scores, flying):
    expert_ids = jnp.arange(flying, dtype=jnp.int32)
    matches = (route_ids[..., None] == expert_ids).astype(jnp.float32)
    hits = jnp.sum(matches, axis=3)
    weighted = (
        ROUTE_SCALE
        * jnp.sum(matches * route_scores[..., None], axis=3)
        / jnp.sum(route_scores, axis=3)[..., None]
    )
    places = jnp.cumsum(hits, axis=2) - 1.0
    slot_ids = jnp.arange(CAP, dtype=jnp.float32)
    placed = hits[..., None] * (places[..., None] == slot_ids).astype(jnp.float32)
    mixed = placed * weighted[..., None]
    earlier = jnp.cumsum(hits, axis=3) - hits
    firsts = placed * (earlier == 0.0).astype(jnp.float32)[..., None]
    flat = hits.shape[:3] + (flying * CAP,)
    return placed.reshape(flat), mixed.reshape(flat), firsts.reshape(flat)


def relay(
    fwd_state,
    rev_state,
    norm_gain,
    w_gate,
    w_up,
    w_down,
    routes_fwd,
    scores_fwd,
    routes_rev,
    scores_rev,
):
    flying = lax.axis_size("g")
    pairs = lax.axis_size("h")
    width = fwd_state.shape[2]
    slots = flying * CAP
    gain_row = norm_gain[0]
    ways = (1, -1)

    def widened(block, axis):
        near = shifted(block, "b", 1)
        return jnp.concatenate(
            [block, shifted(block, "c", 1), near, shifted(near, "c", 1)], axis=axis
        )

    def exchange(blocks):
        return lax.all_to_all(blocks, ("g", "h"), split_axis=0, concat_axis=0, tiled=True)

    def spread(per_expert, stream):
        by_expert = per_expert.reshape(flying, CAP, -1)
        empty = jnp.zeros_like(by_expert)
        both = (by_expert, empty) if stream == 0 else (empty, by_expert)
        return jnp.concatenate(both, axis=1).reshape(2 * slots, -1)

    placed, mixed, firsts = route_tables(
        jnp.stack([routes_fwd[:, 0], routes_rev[:, 0]]),
        jnp.stack([scores_fwd[:, 0], scores_rev[:, 0]]),
        flying,
    )
    placed = placed.swapaxes(2, 3)
    mixing = jnp.einsum("stkr,strq->stkq", placed, mixed, precision=lax.Precision.HIGHEST)
    mixing = [
        [spread(mixing[s, t].T, s).T for t in range(STEPS)] for s in range(2)
    ]
    heard = [shifted(firsts[s].astype(jnp.bfloat16), "pipe", ways[s]) for s in range(2)]
    heard = [value.astype(jnp.float32) for value in heard]
    kept = [1.0 - jnp.sum(value, axis=2) for value in heard]

    def wanted_from(s, t):
        if t == 0:
            return placed[s, 0], None
        return placed[s, t] * kept[s][t - 1], placed[s, t] @ heard[s][t - 1]

    def gathered(rows, changed, from_rows, from_changed):
        found = exact_pick(from_rows, rows)
        if changed is not None:
            found = found + exact_pick(from_changed, changed)
        return found

    def merged_rows(rows, changed, s, t):
        return (
            kept[s][t][:, None] * rows.astype(jnp.float32) + exact_pick(heard[s][t], changed)
        ).astype(jnp.bfloat16)

    gate_cols = widened(w_gate[0], 1)
    up_cols = widened(w_up[0], 1)
    down_rows = widened(w_down[0], 0)

    rows = [fwd_state[0], rev_state[0]]
    base = rows
    changed = [None, None]
    for t in range(STEPS):
        tables = [wanted_from(s, t) for s in range(2)]
        found = sum(
            gathered(
                base[s],
                changed[s],
                spread(tables[s][0], s),
                None if changed[s] is None else spread(tables[s][1], s),
            )
            for s in range(2)
        )
        factor = lax.rsqrt(jnp.mean(found * found, axis=-1, keepdims=True) + EPSILON)
        normed = (found * factor * gain_row).astype(jnp.bfloat16)
        sent = jnp.broadcast_to(
            normed.reshape(flying, 1, 2 * CAP, width), (flying, pairs, 2 * CAP, width)
        ).reshape(flying * pairs, 2 * CAP, width)
        got = exchange(sent)

        if t > 0:
            rows = [merged_rows(base[s], after(changed[s], sent), s, t - 1) for s in range(2)]
        next_base = [shifted(rows[s], "pipe", ways[s]) for s in range(2)]
        own = [exact_pick(placed[s, t], rows[s]) for s in range(2)]

        tok_rows = after(got, *own).reshape(-1, width)
        gate_act = jnp.dot(tok_rows, gate_cols, preferred_element_type=jnp.float32)
        up_act = jnp.dot(tok_rows, up_cols, preferred_element_type=jnp.float32)
        hidden = (jax.nn.silu(gate_act) * up_act).astype(jnp.bfloat16)
        part = jnp.dot(hidden, down_rows, preferred_element_type=jnp.float32)
        part = part.astype(jnp.bfloat16)
        back = exchange(part.reshape(flying * pairs, 2 * CAP, width))

        summed = jnp.sum(
            back.astype(jnp.float32).reshape(flying, pairs, 2 * CAP, width), axis=1
        ).reshape(2 * slots, width)
        changed = [
            shifted(
                (
                    own[s] + jnp.dot(mixing[s][t], summed, precision=lax.Precision.HIGHEST)
                ).astype(jnp.bfloat16),
                "pipe",
                ways[s],
            )
            for s in range(2)
        ]
        base = next_base
    out = [merged_rows(base[s], changed[s], s, STEPS - 1) for s in range(2)]
    return (out[0][None], out[1][None])


def solution(mesh):
    pipe, expert = mesh.devices.shape
    devices = mesh.devices.reshape(pipe, GROUP, expert // (GROUP * PAIRS * 2), PAIRS, 2)
    split = Mesh(devices, ("pipe", "g", "h", "b", "c"))
    column = ("g", "h", "b", "c")
    in_specs = (
        P("pipe", column, None),
        P("pipe", column, None),
        P("pipe", None),
        P("pipe", None, column),
        P("pipe", None, column),
        P("pipe", column, None),
        P(None, "pipe", column, None),
        P(None, "pipe", column, None),
        P(None, "pipe", column, None),
        P(None, "pipe", column, None),
    )
    out_specs = (P("pipe", column, None), P("pipe", column, None))
    return jax.shard_map(relay, mesh=split, in_specs=in_specs, out_specs=out_specs, check_vma=False)
```

profile of v0, /device:TPU:94, one launch (start us, length us, event | category | flops | bytes accessed | tf_op | source)
XLA Modules:
  0.0 328.3 jit_solution(14756960893736177971)
XLA Ops:
  0.6 3.8 %collective-permute-start.6 = (bf16[3584,128]{1,0:T(8,128)(2,1)}, bf16[3584,128]{1,0:T(8,128)(2,1)}, u32[]{:S(2)}, u32[]{:S(2)}) collective-permute-start(bf16[3584,128]{1,0:T(8,128)(2,1)} %bitcast.318), channel_id=1, source_target_pairs={{0,2},{2,0},{1,3},{3,1},{4,6},{6,4},{5,7},{7,5},{8,10},{10,8},{9,1... | collective-permute-start | bytes 2752520 | tf_op jit(solution)/shard_map/ppermute | solution.py:18
  12.8 13.8 %all-to-all-start = ((bf16[8,8,3584]{2,1,0:T(8,128)(2,1)}), bf16[8,8,3584]{2,1,0:T(8,128)(2,1)S(1)}, u32[]{:S(2)}, u32[]{:S(2)}) async-start(bf16[8,8,3584]{2,1,0:T(8,128)(2,1)} %bitcast.24), calls=%async_computation | async-start | bytes 917504 | tf_op jit(solution)/shard_map/all_to_all | solution.py:74
  39.6 29.3 %collective-permute-done.9 = bf16[128,3584]{1,0:T(8,128)(2,1)} collective-permute-done((bf16[128,3584]{1,0:T(8,128)(2,1)}, bf16[128,3584]{1,0:T(8,128)(2,1)}, u32[]{:S(2)}, u32[]{:S(2)}) %collective-permute-start.9) | collective-permute-done | bytes 917536 | tf_op jit(solution)/shard_map/ppermute | solution.py:18
  70.8 16.9 %collective-permute-done.3 = bf16[3584,128]{1,0:T(8,128)(2,1)} collective-permute-done((bf16[3584,128]{1,0:T(8,128)(2,1)}, bf16[3584,128]{1,0:T(8,128)(2,1)}, u32[]{:S(2)}, u32[]{:S(2)}) %collective-permute-start.3) | collective-permute-done | bytes 917536 | tf_op jit(solution)/shard_map/ppermute | solution.py:18
  101.7 5.4 %fusion.2 = bf16[8,8,3584]{2,1,0:T(8,128)(2,1)} fusion(f32[64,512]{1,0:T(8,128)S(1)} %fusion.27, bf16[8,8,3584]{2,1,0:T(8,128)(2,1)S(1)} %all-to-all-done, bf16[128,3584]{1,0:T(8,128)(2,1)} %collective-permute-done.10, bf16[128,3584]{1,0:T(8,128)(2,1)} %collective-permute-done.9, bf16[128,3584]{1,0:T(8,128)(2,1)} %collective-permute-done.8, ...), kind=kOutput, calls=%fused_computation.10 | convolution fusion | flops 499548160 | bytes 8388608 | tf_op jit(solution)/shard_map/dot_general | solution.py:146
  107.0 11.5 %all-to-all-start.1 = ((bf16[8,8,3584]{2,1,0:T(8,128)(2,1)}), bf16[8,8,3584]{2,1,0:T(8,128)(2,1)S(1)}, u32[]{:S(2)}, u32[]{:S(2)}) async-start(bf16[8,8,3584]{2,1,0:T(8,128)(2,1)} %fusion.2), calls=%async_computation.1 | async-start | bytes 917504 | tf_op jit(solution)/shard_map/all_to_all | solution.py:74
  118.8 27.9 %all-to-all-done.1 = bf16[8,8,3584]{2,1,0:T(8,128)(2,1)S(1)} async-done(((bf16[8,8,3584]{2,1,0:T(8,128)(2,1)}), bf16[8,8,3584]{2,1,0:T(8,128)(2,1)S(1)}, u32[]{:S(2)}, u32[]{:S(2)}) %all-to-all-start.1) | async-done | bytes 458784 | tf_op jit(solution)/shard_map/all_to_all | solution.py:74
  150.2 6.5 %collective-permute-start.11 = (bf16[16,3584]{1,0:T(8,128)(2,1)S(1)}, bf16[16,3584]{1,0:T(8,128)(2,1)S(1)}, u32[]{:S(2)}, u32[]{:S(2)}) collective-permute-start(bf16[16,3584]{1,0:T(8,128)(2,1)S(1)} %fusion.11), channel_id=1, source_target_pairs={{0,32},{32,64},{64,96},{96,128},{128,160},{160,192},{192,224},{224... | collective-permute-start | bytes 344072 | tf_op jit(solution)/shard_map/ppermute | solution.py:18
  160.8 4.2 %all-to-all-start.2 = ((bf16[8,8,3584]{2,1,0:T(8,128)(2,1)}), bf16[8,8,3584]{2,1,0:T(8,128)(2,1)S(1)}, u32[]{:S(2)}, u32[]{:S(2)}) async-start(bf16[8,8,3584]{2,1,0:T(8,128)(2,1)} %bitcast.49), calls=%async_computation.2 | async-start | bytes 917504 | tf_op jit(solution)/shard_map/all_to_all | solution.py:74
  166.0 25.4 %all-to-all-done.2 = bf16[8,8,3584]{2,1,0:T(8,128)(2,1)S(1)} async-done(((bf16[8,8,3584]{2,1,0:T(8,128)(2,1)}), bf16[8,8,3584]{2,1,0:T(8,128)(2,1)S(1)}, u32[]{:S(2)}, u32[]{:S(2)}) %all-to-all-start.2) | async-done | bytes 458784 | tf_op jit(solution)/shard_map/all_to_all | solution.py:74
  193.8 5.1 %fusion.3 = bf16[8,8,3584]{2,1,0:T(8,128)(2,1)} fusion(f32[64,512]{1,0:T(8,128)S(1)} %fusion.23, bf16[8,8,3584]{2,1,0:T(8,128)(2,1)S(1)} %all-to-all-done.2, bf16[128,3584]{1,0:T(8,128)(2,1)} %collective-permute-done.10, bf16[128,3584]{1,0:T(8,128)(2,1)} %collective-permute-done.9, bf16[128,3584]{1,0:T(8,128)(2,1)} %collective-permute-done.8, ...), kind=kOutput, calls=%fused_computation.11 | convolution fusion | flops 499548160 | bytes 8388608 | tf_op jit(solution)/shard_map/dot_general | solution.py:146
  198.9 4.7 %all-to-all-start.3 = ((bf16[8,8,3584]{2,1,0:T(8,128)(2,1)}), bf16[8,8,3584]{2,1,0:T(8,128)(2,1)S(1)}, u32[]{:S(2)}, u32[]{:S(2)}) async-start(bf16[8,8,3584]{2,1,0:T(8,128)(2,1)} %fusion.3), calls=%async_computation.3 | async-start | bytes 917504 | tf_op jit(solution)/shard_map/all_to_all | solution.py:74
  204.0 7.3 %collective-permute-start.15 = (bf16[64,3584]{1,0:T(8,128)(2,1)S(1)}, bf16[64,3584]{1,0:T(8,128)(2,1)S(1)}, u32[]{:S(2)}, u32[]{:S(2)}) collective-permute-start(bf16[64,3584]{1,0:T(8,128)(2,1)S(1)} %add_convert_fusion.5), channel_id=1, source_target_pairs={{0,32},{32,64},{64,96},{96,128},{128,160},{160,192},{192,224},{224... | collective-permute-start | bytes 1376264 | tf_op jit(solution)/shard_map/ppermute | solution.py:18
  213.2 8.0 %all-to-all-done.3 = bf16[8,8,3584]{2,1,0:T(8,128)(2,1)S(1)} async-done(((bf16[8,8,3584]{2,1,0:T(8,128)(2,1)}), bf16[8,8,3584]{2,1,0:T(8,128)(2,1)S(1)}, u32[]{:S(2)}, u32[]{:S(2)}) %all-to-all-start.3) | async-done | bytes 458784 | tf_op jit(solution)/shard_map/all_to_all | solution.py:74
  221.7 4.4 %collective-permute-start.18 = (bf16[16,3584]{1,0:T(8,128)(2,1)S(1)}, bf16[16,3584]{1,0:T(8,128)(2,1)S(1)}, u32[]{:S(2)}, u32[]{:S(2)}) collective-permute-start(bf16[16,3584]{1,0:T(8,128)(2,1)S(1)} %fusion.14), channel_id=1, source_target_pairs={{0,480},{32,0},{64,32},{96,64},{128,96},{160,128},{192,160},{224,1... | collective-permute-start | bytes 344072 | tf_op jit(solution)/shard_map/ppermute | solution.py:18
  226.6 7.3 %collective-permute-start.16 = (bf16[16,3584]{1,0:T(8,128)(2,1)S(1)}, bf16[16,3584]{1,0:T(8,128)(2,1)S(1)}, u32[]{:S(2)}, u32[]{:S(2)}) collective-permute-start(bf16[16,3584]{1,0:T(8,128)(2,1)S(1)} %fusion.13), channel_id=1, source_target_pairs={{0,32},{32,64},{64,96},{96,128},{128,160},{160,192},{192,224},{224... | collective-permute-start | bytes 344072 | tf_op jit(solution)/shard_map/ppermute | solution.py:18
  237.9 11.3 %all-to-all-start.4 = ((bf16[8,8,3584]{2,1,0:T(8,128)(2,1)}), bf16[8,8,3584]{2,1,0:T(8,128)(2,1)S(1)}, u32[]{:S(2)}, u32[]{:S(2)}) async-start(bf16[8,8,3584]{2,1,0:T(8,128)(2,1)} %bitcast.75), calls=%async_computation.4 | async-start | bytes 917504 | tf_op jit(solution)/shard_map/all_to_all | solution.py:74
  250.1 23.0 %all-to-all-done.4 = bf16[8,8,3584]{2,1,0:T(8,128)(2,1)S(1)} async-done(((bf16[8,8,3584]{2,1,0:T(8,128)(2,1)}), bf16[8,8,3584]{2,1,0:T(8,128)(2,1)S(1)}, u32[]{:S(2)}, u32[]{:S(2)}) %all-to-all-start.4) | async-done | bytes 458784 | tf_op jit(solution)/shard_map/all_to_all | solution.py:74
  275.6 5.3 %fusion.4 = bf16[8,8,3584]{2,1,0:T(8,128)(2,1)} fusion(f32[64,512]{1,0:T(8,128)S(1)} %fusion.19, bf16[8,8,3584]{2,1,0:T(8,128)(2,1)S(1)} %all-to-all-done.4, bf16[128,3584]{1,0:T(8,128)(2,1)} %collective-permute-done.10, bf16[128,3584]{1,0:T(8,128)(2,1)} %collective-permute-done.9, bf16[128,3584]{1,0:T(8,128)(2,1)} %collective-permute-done.8, ...), kind=kOutput, calls=%fused_computation.12 | convolution fusion | flops 499548160 | bytes 8388608 | tf_op jit(solution)/shard_map/dot_general | solution.py:146
  280.9 4.2 %all-to-all-start.5 = ((bf16[8,8,3584]{2,1,0:T(8,128)(2,1)}), bf16[8,8,3584]{2,1,0:T(8,128)(2,1)S(1)}, u32[]{:S(2)}, u32[]{:S(2)}) async-start(bf16[8,8,3584]{2,1,0:T(8,128)(2,1)} %fusion.4), calls=%async_computation.5 | async-start | bytes 917504 | tf_op jit(solution)/shard_map/all_to_all | solution.py:74
  285.3 8.0 %collective-permute-start.19 = (bf16[64,3584]{1,0:T(8,128)(2,1)S(1)}, bf16[64,3584]{1,0:T(8,128)(2,1)S(1)}, u32[]{:S(2)}, u32[]{:S(2)}) collective-permute-start(bf16[64,3584]{1,0:T(8,128)(2,1)S(1)} %add_convert_fusion.3), channel_id=1, source_target_pairs={{0,32},{32,64},{64,96},{96,128},{128,160},{160,192},{192,224},{224... | collective-permute-start | bytes 1376264 | tf_op jit(solution)/shard_map/ppermute | solution.py:18
  295.2 13.0 %all-to-all-done.5 = bf16[8,8,3584]{2,1,0:T(8,128)(2,1)S(1)} async-done(((bf16[8,8,3584]{2,1,0:T(8,128)(2,1)}), bf16[8,8,3584]{2,1,0:T(8,128)(2,1)S(1)}, u32[]{:S(2)}, u32[]{:S(2)}) %all-to-all-start.5) | async-done | bytes 458784 | tf_op jit(solution)/shard_map/all_to_all | solution.py:74
  308.7 8.1 %collective-permute-start.20 = (bf16[16,3584]{1,0:T(8,128)(2,1)S(1)}, bf16[16,3584]{1,0:T(8,128)(2,1)S(1)}, u32[]{:S(2)}, u32[]{:S(2)}) collective-permute-start(bf16[16,3584]{1,0:T(8,128)(2,1)S(1)} %fusion.15), channel_id=1, source_target_pairs={{0,32},{32,64},{64,96},{96,128},{128,160},{160,192},{192,224},{224... | collective-permute-start | bytes 344072 | tf_op jit(solution)/shard_map/ppermute | solution.py:18
  320.2 7.0 %collective-permute-done.22 = bf16[16,3584]{1,0:T(8,128)(2,1)S(1)} collective-permute-done((bf16[16,3584]{1,0:T(8,128)(2,1)S(1)}, bf16[16,3584]{1,0:T(8,128)(2,1)S(1)}, u32[]{:S(2)}, u32[]{:S(2)}) %collective-permute-start.22) | collective-permute-done | bytes 114720 | tf_op jit(solution)/shard_map/ppermute | solution.py:18
  (131 shorter events, 65.6 us)
Async XLA Ops:
  0.6 32.2 %collective-permute-start.6 = (bf16[3584,128]{1,0:T(8,128)(2,1)}, bf16[3584,128]{1,0:T(8,128)(2,1)}, u32[]{:S(2)}, u32[]{:S(2)}) collective-permute-start(bf16[3584,128]{1,0:T(8,128)(2,1)} %bitcast.318), channel_id=1, source_target_pairs={{0,2},{2,0},{1,3},{3,1},{4,6},{6,4},{5,7},{7,5},{8,10},{10,8},{9,1... | collective-permute-start | bytes 2752520 | tf_op jit(solution)/shard_map/ppermute | solution.py:18
  4.5 33.2 %collective-permute-start.5 = (bf16[3584,128]{1,0:T(8,128)(2,1)}, bf16[3584,128]{1,0:T(8,128)(2,1)}, u32[]{:S(2)}, u32[]{:S(2)}) collective-permute-start(bf16[3584,128]{1,0:T(8,128)(2,1)} %bitcast.319), channel_id=1, source_target_pairs={{0,1},{1,0},{2,3},{3,2},{4,5},{5,4},{6,7},{7,6},{8,9},{9,8},{10,11... | collective-permute-start | bytes 2752520 | tf_op jit(solution)/shard_map/ppermute | solution.py:18
  8.6 26.6 %collective-permute-start = (bf16[3,64,16]{1,2,0:T(8,128)(2,1)S(1)}, bf16[3,64,16]{1,2,0:T(8,128)(2,1)S(1)}, u32[]{:S(2)}, u32[]{:S(2)}) collective-permute-start(bf16[3,64,16]{1,2,0:T(8,128)(2,1)S(1)} %bitcast.315), channel_id=1, source_target_pairs={{0,32},{32,64},{64,96},{96,128},{128,160},{160,192},{192,224},{224... | collective-permute-start | bytes 18440 | tf_op jit(solution)/shard_map/ppermute | solution.py:18
  12.8 76.9 %all-to-all-start = ((bf16[8,8,3584]{2,1,0:T(8,128)(2,1)}), bf16[8,8,3584]{2,1,0:T(8,128)(2,1)S(1)}, u32[]{:S(2)}, u32[]{:S(2)}) async-start(bf16[8,8,3584]{2,1,0:T(8,128)(2,1)} %bitcast.24), calls=%async_computation | async-start | bytes 917504 | tf_op jit(solution)/shard_map/all_to_all | solution.py:74
  26.6 42.3 %collective-permute-start.9 = (bf16[128,3584]{1,0:T(8,128)(2,1)}, bf16[128,3584]{1,0:T(8,128)(2,1)}, u32[]{:S(2)}, u32[]{:S(2)}) collective-permute-start(bf16[128,3584]{1,0:T(8,128)(2,1)} %bitcast.323), channel_id=1, source_target_pairs={{0,2},{2,0},{1,3},{3,1},{4,6},{6,4},{5,7},{7,5},{8,10},{10,8},{9,1... | collective-permute-start | bytes 2752520 | tf_op jit(solution)/shard_map/ppermute | solution.py:18
  29.5 58.1 %collective-permute-start.3 = (bf16[3584,128]{1,0:T(8,128)(2,1)}, bf16[3584,128]{1,0:T(8,128)(2,1)}, u32[]{:S(2)}, u32[]{:S(2)}) collective-permute-start(bf16[3584,128]{1,0:T(8,128)(2,1)} %bitcast.328), channel_id=1, source_target_pairs={{0,2},{2,0},{1,3},{3,1},{4,6},{6,4},{5,7},{7,5},{8,10},{10,8},{9,1... | collective-permute-start | bytes 2752520 | tf_op jit(solution)/shard_map/ppermute | solution.py:18
  32.8 56.8 %collective-permute-start.7 = (bf16[3584,128]{1,0:T(8,128)(2,1)}, bf16[3584,128]{1,0:T(8,128)(2,1)}, u32[]{:S(2)}, u32[]{:S(2)}) collective-permute-start(bf16[3584,128]{1,0:T(8,128)(2,1)} %collective-permute-done.6), channel_id=1, source_target_pairs={{0,1},{1,0},{2,3},{3,2},{4,5},{5,4},{6,7},{7,6},{8,9},{9,8},{10,11... | collective-permute-start | bytes 2752520 | tf_op jit(solution)/shard_map/ppermute | solution.py:18
  35.2 60.2 %collective-permute-start.8 = (bf16[128,3584]{1,0:T(8,128)(2,1)}, bf16[128,3584]{1,0:T(8,128)(2,1)}, u32[]{:S(2)}, u32[]{:S(2)}) collective-permute-start(bf16[128,3584]{1,0:T(8,128)(2,1)} %bitcast.324), channel_id=1, source_target_pairs={{0,1},{1,0},{2,3},{3,2},{4,5},{5,4},{6,7},{7,6},{8,9},{9,8},{10,11... | collective-permute-start | bytes 2752520 | tf_op jit(solution)/shard_map/ppermute | solution.py:18
  37.6 60.3 %collective-permute-start.2 = (bf16[3584,128]{1,0:T(8,128)(2,1)}, bf16[3584,128]{1,0:T(8,128)(2,1)}, u32[]{:S(2)}, u32[]{:S(2)}) collective-permute-start(bf16[3584,128]{1,0:T(8,128)(2,1)} %bitcast.329), channel_id=1, source_target_pairs={{0,1},{1,0},{2,3},{3,2},{4,5},{5,4},{6,7},{7,6},{8,9},{9,8},{10,11... | collective-permute-start | bytes 2752520 | tf_op jit(solution)/shard_map/ppermute | solution.py:18
  68.9 32.8 %collective-permute-start.10 = (bf16[128,3584]{1,0:T(8,128)(2,1)}, bf16[128,3584]{1,0:T(8,128)(2,1)}, u32[]{:S(2)}, u32[]{:S(2)}) collective-permute-start(bf16[128,3584]{1,0:T(8,128)(2,1)} %collective-permute-done.9), channel_id=1, source_target_pairs={{0,1},{1,0},{2,3},{3,2},{4,5},{5,4},{6,7},{7,6},{8,9},{9,8},{10,11... | collective-permute-start | bytes 2752520 | tf_op jit(solution)/shard_map/ppermute | solution.py:18
  87.7 14.0 %collective-permute-start.4 = (bf16[3584,128]{1,0:T(8,128)(2,1)}, bf16[3584,128]{1,0:T(8,128)(2,1)}, u32[]{:S(2)}, u32[]{:S(2)}) collective-permute-start(bf16[3584,128]{1,0:T(8,128)(2,1)} %collective-permute-done.3), channel_id=1, source_target_pairs={{0,1},{1,0},{2,3},{3,2},{4,5},{5,4},{6,7},{7,6},{8,9},{9,8},{10,11... | collective-permute-start | bytes 2752520 | tf_op jit(solution)/shard_map/ppermute | solution.py:18
  89.6 69.9 %collective-permute-start.1 = (bf16[64,3584]{1,0:T(8,128)(2,1)S(1)}, bf16[64,3584]{1,0:T(8,128)(2,1)S(1)}, u32[]{:S(2)}, u32[]{:S(2)}) collective-permute-start(bf16[64,3584]{1,0:T(8,128)(2,1)S(1)} %bitcast.289), channel_id=1, source_target_pairs={{0,32},{32,64},{64,96},{96,128},{128,160},{160,192},{192,224},{224... | collective-permute-start | bytes 1376264 | tf_op jit(solution)/shard_map/ppermute | solution.py:18
  95.4 23.0 %collective-permute-start.12 = (bf16[3,64,16]{1,2,0:T(8,128)(2,1)S(1)}, bf16[3,64,16]{1,2,0:T(8,128)(2,1)S(1)}, u32[]{:S(2)}, u32[]{:S(2)}) collective-permute-start(bf16[3,64,16]{1,2,0:T(8,128)(2,1)S(1)} %bitcast.314), channel_id=1, source_target_pairs={{0,480},{32,0},{64,32},{96,64},{128,96},{160,128},{192,160},{224,1... | collective-permute-start | bytes 18440 | tf_op jit(solution)/shard_map/ppermute | solution.py:18
  98.0 61.3 %collective-permute-start.13 = (bf16[64,3584]{1,0:T(8,128)(2,1)S(1)}, bf16[64,3584]{1,0:T(8,128)(2,1)S(1)}, u32[]{:S(2)}, u32[]{:S(2)}) collective-permute-start(bf16[64,3584]{1,0:T(8,128)(2,1)S(1)} %bitcast.290), channel_id=1, source_target_pairs={{0,480},{32,0},{64,32},{96,64},{128,96},{160,128},{192,160},{224,1... | collective-permute-start | bytes 1376264 | tf_op jit(solution)/shard_map/ppermute | solution.py:18
  107.0 39.7 %all-to-all-start.1 = ((bf16[8,8,3584]{2,1,0:T(8,128)(2,1)}), bf16[8,8,3584]{2,1,0:T(8,128)(2,1)S(1)}, u32[]{:S(2)}, u32[]{:S(2)}) async-start(bf16[8,8,3584]{2,1,0:T(8,128)(2,1)} %fusion.2), calls=%async_computation.1 | async-start | bytes 917504 | tf_op jit(solution)/shard_map/all_to_all | solution.py:74
  160.8 30.6 %all-to-all-start.2 = ((bf16[8,8,3584]{2,1,0:T(8,128)(2,1)}), bf16[8,8,3584]{2,1,0:T(8,128)(2,1)S(1)}, u32[]{:S(2)}, u32[]{:S(2)}) async-start(bf16[8,8,3584]{2,1,0:T(8,128)(2,1)} %bitcast.49), calls=%async_computation.2 | async-start | bytes 917504 | tf_op jit(solution)/shard_map/all_to_all | solution.py:74
  198.9 22.3 %all-to-all-start.3 = ((bf16[8,8,3584]{2,1,0:T(8,128)(2,1)}), bf16[8,8,3584]{2,1,0:T(8,128)(2,1)S(1)}, u32[]{:S(2)}, u32[]{:S(2)}) async-start(bf16[8,8,3584]{2,1,0:T(8,128)(2,1)} %fusion.3), calls=%async_computation.3 | async-start | bytes 917504 | tf_op jit(solution)/shard_map/all_to_all | solution.py:74
  204.0 32.6 %collective-permute-start.15 = (bf16[64,3584]{1,0:T(8,128)(2,1)S(1)}, bf16[64,3584]{1,0:T(8,128)(2,1)S(1)}, u32[]{:S(2)}, u32[]{:S(2)}) collective-permute-start(bf16[64,3584]{1,0:T(8,128)(2,1)S(1)} %add_convert_fusion.5), channel_id=1, source_target_pairs={{0,32},{32,64},{64,96},{96,128},{128,160},{160,192},{192,224},{224... | collective-permute-start | bytes 1376264 | tf_op jit(solution)/shard_map/ppermute | solution.py:18
  211.3 25.1 %collective-permute-start.17 = (bf16[64,3584]{1,0:T(8,128)(2,1)S(1)}, bf16[64,3584]{1,0:T(8,128)(2,1)S(1)}, u32[]{:S(2)}, u32[]{:S(2)}) collective-permute-start(bf16[64,3584]{1,0:T(8,128)(2,1)S(1)} %add_convert_fusion.4), channel_id=1, source_target_pairs={{0,480},{32,0},{64,32},{96,64},{128,96},{160,128},{192,160},{224,1... | collective-permute-start | bytes 1376264 | tf_op jit(solution)/shard_map/ppermute | solution.py:18
  221.7 12.5 %collective-permute-start.18 = (bf16[16,3584]{1,0:T(8,128)(2,1)S(1)}, bf16[16,3584]{1,0:T(8,128)(2,1)S(1)}, u32[]{:S(2)}, u32[]{:S(2)}) collective-permute-start(bf16[16,3584]{1,0:T(8,128)(2,1)S(1)} %fusion.14), channel_id=1, source_target_pairs={{0,480},{32,0},{64,32},{96,64},{128,96},{160,128},{192,160},{224,1... | collective-permute-start | bytes 344072 | tf_op jit(solution)/shard_map/ppermute | solution.py:18
  237.9 35.3 %all-to-all-start.4 = ((bf16[8,8,3584]{2,1,0:T(8,128)(2,1)}), bf16[8,8,3584]{2,1,0:T(8,128)(2,1)S(1)}, u32[]{:S(2)}, u32[]{:S(2)}) async-start(bf16[8,8,3584]{2,1,0:T(8,128)(2,1)} %bitcast.75), calls=%async_computation.4 | async-start | bytes 917504 | tf_op jit(solution)/shard_map/all_to_all | solution.py:74
  280.9 27.3 %all-to-all-start.5 = ((bf16[8,8,3584]{2,1,0:T(8,128)(2,1)}), bf16[8,8,3584]{2,1,0:T(8,128)(2,1)S(1)}, u32[]{:S(2)}, u32[]{:S(2)}) async-start(bf16[8,8,3584]{2,1,0:T(8,128)(2,1)} %fusion.4), calls=%async_computation.5 | async-start | bytes 917504 | tf_op jit(solution)/shard_map/all_to_all | solution.py:74
  285.3 33.9 %collective-permute-start.19 = (bf16[64,3584]{1,0:T(8,128)(2,1)S(1)}, bf16[64,3584]{1,0:T(8,128)(2,1)S(1)}, u32[]{:S(2)}, u32[]{:S(2)}) collective-permute-start(bf16[64,3584]{1,0:T(8,128)(2,1)S(1)} %add_convert_fusion.3), channel_id=1, source_target_pairs={{0,32},{32,64},{64,96},{96,128},{128,160},{160,192},{192,224},{224... | collective-permute-start | bytes 1376264 | tf_op jit(solution)/shard_map/ppermute | solution.py:18
  293.3 26.9 %collective-permute-start.21 = (bf16[64,3584]{1,0:T(8,128)(2,1)S(1)}, bf16[64,3584]{1,0:T(8,128)(2,1)S(1)}, u32[]{:S(2)}, u32[]{:S(2)}) collective-permute-start(bf16[64,3584]{1,0:T(8,128)(2,1)S(1)} %add_convert_fusion.2), channel_id=1, source_target_pairs={{0,480},{32,0},{64,32},{96,64},{128,96},{160,128},{192,160},{224,1... | collective-permute-start | bytes 1376264 | tf_op jit(solution)/shard_map/ppermute | solution.py:18
  (9 other events, 84.0 us)
where the time goes:
time: 330 us; the launch traced here: 328 us
  waiting for transfers between devices  155 us (47%)
  starting transfers between devices  133 us (40%)
  matrix products  33 us (10%)
  local copies, waits for them, and re-layouts  3.6 us (1%)
    all_to_all x6, waiting for transfers between devices, exchange(): lax.all_to_all(blocks, ('g', 'h'), split_axis=0, concat_axis=0, tiled=True)  97.3 us
    ppermute x23, starting transfers between devices, shifted(): return lax.ppermute(value, axis, pairs)  83.3 us
    ppermute x23, waiting for transfers between devices, shifted(): return lax.ppermute(value, axis, pairs)  57.5 us
    all_to_all x6, starting transfers between devices, exchange(): lax.all_to_all(blocks, ('g', 'h'), split_axis=0, concat_axis=0, tiled=True)  49.6 us
    dot_general x3, matrix products, relay(): part = jnp.dot(hidden, down_rows, preferred_element_type=jnp.float32)  15.8 us
    dot_general x3, matrix products, relay(): up_act = jnp.dot(tok_rows, up_cols, preferred_element_type=jnp.float32)  7.33 us
    dot_general x22, matrix products, exact_pick(): jnp.dot(table.astype(jnp.bfloat16), rows, preferred_element_type=jnp.floa...  6.68 us
  transfers between devices with their start and end apart: 29, of which 12 were waited for; matrix products, arithmetic and copies ran while one was open for 6% of the time, Pallas kernels for 0%

commit v1 on v0

--- a/solution.py
+++ b/solution.py
@@ -66,9 +66,8 @@
 
     def widened(block, axis):
         near = shifted(block, "b", 1)
-        return jnp.concatenate(
-            [block, shifted(block, "c", 1), near, shifted(near, "c", 1)], axis=axis
-        )
+        other = shifted(block, "c", 1)
+        return jnp.concatenate([block, other, near, shifted(near, "c", 1)], axis=axis)
 
     def exchange(blocks):
         return lax.all_to_all(blocks, ("g", "h"), split_axis=0, concat_axis=0, tiled=True)
@@ -143,8 +142,7 @@
         gate_act = jnp.dot(tok_rows, gate_cols, preferred_element_type=jnp.float32)
         up_act = jnp.dot(tok_rows, up_cols, preferred_element_type=jnp.float32)
         hidden = (jax.nn.silu(gate_act) * up_act).astype(jnp.bfloat16)
-        part = jnp.dot(hidden, down_rows, preferred_element_type=jnp.float32)
-        part = part.astype(jnp.bfloat16)
+        part = jnp.dot(hidden, down_rows, preferred_element_type=jnp.float32).astype(jnp.bfloat16)
         back = exchange(part.reshape(flying * pairs, 2 * CAP, width))
 
         summed = jnp.sum(

time: 330 us -> 330 us (level)
  no operation moved by 1% of the time
where the time goes in v1:
time: 330 us; the launch traced here: 328 us
  waiting for transfers between devices  155 us (47%)
  starting transfers between devices  133 us (40%)
  matrix products  33 us (10%)
  local copies, waits for them, and re-layouts  3.6 us (1%)
    all_to_all x6, waiting for transfers between devices, exchange(): lax.all_to_all(blocks, ('g', 'h'), split_axis=0, concat_axis=0, tiled=True)  97.3 us
    ppermute x23, starting transfers between devices, shifted(): return lax.ppermute(value, axis, pairs)  83.3 us
    ppermute x23, waiting for transfers between devices, shifted(): return lax.ppermute(value, axis, pairs)  57.5 us
    all_to_all x6, starting transfers between devices, exchange(): lax.all_to_all(blocks, ('g', 'h'), split_axis=0, concat_axis=0, tiled=True)  49.6 us
    dot_general x3, matrix products, relay(): jnp.dot(hidden, down_rows, preferred_element_type=jnp.float32)  15.8 us
    dot_general x3, matrix products, relay(): up_act = jnp.dot(tok_rows, up_cols, preferred_element_type=jnp.float32)  7.33 us
    dot_general x22, matrix products, exact_pick(): jnp.dot(table.astype(jnp.bfloat16), rows, preferred_element_type=jnp.floa...  6.68 us
  transfers between devices with their start and end apart: 29, of which 12 were waited for; matrix products, arithmetic and copies ran while one was open for 6% of the time, Pallas kernels for 0%

profile of v1, /device:TPU:94, one launch (start us, length us, event | category | flops | bytes accessed | tf_op | source)
XLA Modules:
  0.0 328.3 jit_solution(14756960893736177971)
XLA Ops:
  0.6 3.8 %collective-permute-start.6 = (bf16[3584,128]{1,0:T(8,128)(2,1)}, bf16[3584,128]{1,0:T(8,128)(2,1)}, u32[]{:S(2)}, u32[]{:S(2)}) collective-permute-start(bf16[3584,128]{1,0:T(8,128)(2,1)} %bitcast.318), channel_id=1, source_target_pairs={{0,2},{2,0},{1,3},{3,1},{4,6},{6,4},{5,7},{7,5},{8,10},{10,8},{9,1... | collective-permute-start | bytes 2752520 | tf_op jit(solution)/shard_map/ppermute | solution.py:18
  12.8 13.8 %all-to-all-start = ((bf16[8,8,3584]{2,1,0:T(8,128)(2,1)}), bf16[8,8,3584]{2,1,0:T(8,128)(2,1)S(1)}, u32[]{:S(2)}, u32[]{:S(2)}) async-start(bf16[8,8,3584]{2,1,0:T(8,128)(2,1)} %bitcast.24), calls=%async_computation | async-start | bytes 917504 | tf_op jit(solution)/shard_map/all_to_all | solution.py:73
  39.6 29.3 %collective-permute-done.9 = bf16[128,3584]{1,0:T(8,128)(2,1)} collective-permute-done((bf16[128,3584]{1,0:T(8,128)(2,1)}, bf16[128,3584]{1,0:T(8,128)(2,1)}, u32[]{:S(2)}, u32[]{:S(2)}) %collective-permute-start.9) | collective-permute-done | bytes 917536 | tf_op jit(solution)/shard_map/ppermute | solution.py:18
  70.8 16.9 %collective-permute-done.3 = bf16[3584,128]{1,0:T(8,128)(2,1)} collective-permute-done((bf16[3584,128]{1,0:T(8,128)(2,1)}, bf16[3584,128]{1,0:T(8,128)(2,1)}, u32[]{:S(2)}, u32[]{:S(2)}) %collective-permute-start.3) | collective-permute-done | bytes 917536 | tf_op jit(solution)/shard_map/ppermute | solution.py:18
  101.7 5.4 %fusion.2 = bf16[8,8,3584]{2,1,0:T(8,128)(2,1)} fusion(f32[64,512]{1,0:T(8,128)S(1)} %fusion.27, bf16[8,8,3584]{2,1,0:T(8,128)(2,1)S(1)} %all-to-all-done, bf16[128,3584]{1,0:T(8,128)(2,1)} %collective-permute-done.10, bf16[128,3584]{1,0:T(8,128)(2,1)} %collective-permute-done.9, bf16[128,3584]{1,0:T(8,128)(2,1)} %collective-permute-done.8, ...), kind=kOutput, calls=%fused_computation.10 | convolution fusion | flops 499548160 | bytes 8388608 | tf_op jit(solution)/shard_map/dot_general | solution.py:145
  107.0 11.5 %all-to-all-start.1 = ((bf16[8,8,3584]{2,1,0:T(8,128)(2,1)}), bf16[8,8,3584]{2,1,0:T(8,128)(2,1)S(1)}, u32[]{:S(2)}, u32[]{:S(2)}) async-start(bf16[8,8,3584]{2,1,0:T(8,128)(2,1)} %fusion.2), calls=%async_computation.1 | async-start | bytes 917504 | tf_op jit(solution)/shard_map/all_to_all | solution.py:73
  118.8 27.9 %all-to-all-done.1 = bf16[8,8,3584]{2,1,0:T(8,128)(2,1)S(1)} async-done(((bf16[8,8,3584]{2,1,0:T(8,128)(2,1)}), bf16[8,8,3584]{2,1,0:T(8,128)(2,1)S(1)}, u32[]{:S(2)}, u32[]{:S(2)}) %all-to-all-start.1) | async-done | bytes 458784 | tf_op jit(solution)/shard_map/all_to_all | solution.py:73
  150.2 6.5 %collective-permute-start.11 = (bf16[16,3584]{1,0:T(8,128)(2,1)S(1)}, bf16[16,3584]{1,0:T(8,128)(2,1)S(1)}, u32[]{:S(2)}, u32[]{:S(2)}) collective-permute-start(bf16[16,3584]{1,0:T(8,128)(2,1)S(1)} %fusion.11), channel_id=1, source_target_pairs={{0,32},{32,64},{64,96},{96,128},{128,160},{160,192},{192,224},{224... | collective-permute-start | bytes 344072 | tf_op jit(solution)/shard_map/ppermute | solution.py:18
  160.8 4.2 %all-to-all-start.2 = ((bf16[8,8,3584]{2,1,0:T(8,128)(2,1)}), bf16[8,8,3584]{2,1,0:T(8,128)(2,1)S(1)}, u32[]{:S(2)}, u32[]{:S(2)}) async-start(bf16[8,8,3584]{2,1,0:T(8,128)(2,1)} %bitcast.49), calls=%async_computation.2 | async-start | bytes 917504 | tf_op jit(solution)/shard_map/all_to_all | solution.py:73
  166.0 25.4 %all-to-all-done.2 = bf16[8,8,3584]{2,1,0:T(8,128)(2,1)S(1)} async-done(((bf16[8,8,3584]{2,1,0:T(8,128)(2,1)}), bf16[8,8,3584]{2,1,0:T(8,128)(2,1)S(1)}, u32[]{:S(2)}, u32[]{:S(2)}) %all-to-all-start.2) | async-done | bytes 458784 | tf_op jit(solution)/shard_map/all_to_all | solution.py:73
  193.8 5.1 %fusion.3 = bf16[8,8,3584]{2,1,0:T(8,128)(2,1)} fusion(f32[64,512]{1,0:T(8,128)S(1)} %fusion.23, bf16[8,8,3584]{2,1,0:T(8,128)(2,1)S(1)} %all-to-all-done.2, bf16[128,3584]{1,0:T(8,128)(2,1)} %collective-permute-done.10, bf16[128,3584]{1,0:T(8,128)(2,1)} %collective-permute-done.9, bf16[128,3584]{1,0:T(8,128)(2,1)} %collective-permute-done.8, ...), kind=kOutput, calls=%fused_computation.11 | convolution fusion | flops 499548160 | bytes 8388608 | tf_op jit(solution)/shard_map/dot_general | solution.py:145
  198.9 4.7 %all-to-all-start.3 = ((bf16[8,8,3584]{2,1,0:T(8,128)(2,1)}), bf16[8,8,3584]{2,1,0:T(8,128)(2,1)S(1)}, u32[]{:S(2)}, u32[]{:S(2)}) async-start(bf16[8,8,3584]{2,1,0:T(8,128)(2,1)} %fusion.3), calls=%async_computation.3 | async-start | bytes 917504 | tf_op jit(solution)/shard_map/all_to_all | solution.py:73
  204.0 7.3 %collective-permute-start.15 = (bf16[64,3584]{1,0:T(8,128)(2,1)S(1)}, bf16[64,3584]{1,0:T(8,128)(2,1)S(1)}, u32[]{:S(2)}, u32[]{:S(2)}) collective-permute-start(bf16[64,3584]{1,0:T(8,128)(2,1)S(1)} %add_convert_fusion.5), channel_id=1, source_target_pairs={{0,32},{32,64},{64,96},{96,128},{128,160},{160,192},{192,224},{224... | collective-permute-start | bytes 1376264 | tf_op jit(solution)/shard_map/ppermute | solution.py:18
  213.2 8.0 %all-to-all-done.3 = bf16[8,8,3584]{2,1,0:T(8,128)(2,1)S(1)} async-done(((bf16[8,8,3584]{2,1,0:T(8,128)(2,1)}), bf16[8,8,3584]{2,1,0:T(8,128)(2,1)S(1)}, u32[]{:S(2)}, u32[]{:S(2)}) %all-to-all-start.3) | async-done | bytes 458784 | tf_op jit(solution)/shard_map/all_to_all | solution.py:73
  221.7 4.4 %collective-permute-start.18 = (bf16[16,3584]{1,0:T(8,128)(2,1)S(1)}, bf16[16,3584]{1,0:T(8,128)(2,1)S(1)}, u32[]{:S(2)}, u32[]{:S(2)}) collective-permute-start(bf16[16,3584]{1,0:T(8,128)(2,1)S(1)} %fusion.14), channel_id=1, source_target_pairs={{0,480},{32,0},{64,32},{96,64},{128,96},{160,128},{192,160},{224,1... | collective-permute-start | bytes 344072 | tf_op jit(solution)/shard_map/ppermute | solution.py:18
  226.6 7.3 %collective-permute-start.16 = (bf16[16,3584]{1,0:T(8,128)(2,1)S(1)}, bf16[16,3584]{1,0:T(8,128)(2,1)S(1)}, u32[]{:S(2)}, u32[]{:S(2)}) collective-permute-start(bf16[16,3584]{1,0:T(8,128)(2,1)S(1)} %fusion.13), channel_id=1, source_target_pairs={{0,32},{32,64},{64,96},{96,128},{128,160},{160,192},{192,224},{224... | collective-permute-start | bytes 344072 | tf_op jit(solution)/shard_map/ppermute | solution.py:18
  237.9 11.3 %all-to-all-start.4 = ((bf16[8,8,3584]{2,1,0:T(8,128)(2,1)}), bf16[8,8,3584]{2,1,0:T(8,128)(2,1)S(1)}, u32[]{:S(2)}, u32[]{:S(2)}) async-start(bf16[8,8,3584]{2,1,0:T(8,128)(2,1)} %bitcast.75), calls=%async_computation.4 | async-start | bytes 917504 | tf_op jit(solution)/shard_map/all_to_all | solution.py:73
  250.1 23.0 %all-to-all-done.4 = bf16[8,8,3584]{2,1,0:T(8,128)(2,1)S(1)} async-done(((bf16[8,8,3584]{2,1,0:T(8,128)(2,1)}), bf16[8,8,3584]{2,1,0:T(8,128)(2,1)S(1)}, u32[]{:S(2)}, u32[]{:S(2)}) %all-to-all-start.4) | async-done | bytes 458784 | tf_op jit(solution)/shard_map/all_to_all | solution.py:73
  275.6 5.3 %fusion.4 = bf16[8,8,3584]{2,1,0:T(8,128)(2,1)} fusion(f32[64,512]{1,0:T(8,128)S(1)} %fusion.19, bf16[8,8,3584]{2,1,0:T(8,128)(2,1)S(1)} %all-to-all-done.4, bf16[128,3584]{1,0:T(8,128)(2,1)} %collective-permute-done.10, bf16[128,3584]{1,0:T(8,128)(2,1)} %collective-permute-done.9, bf16[128,3584]{1,0:T(8,128)(2,1)} %collective-permute-done.8, ...), kind=kOutput, calls=%fused_computation.12 | convolution fusion | flops 499548160 | bytes 8388608 | tf_op jit(solution)/shard_map/dot_general | solution.py:145
  280.9 4.2 %all-to-all-start.5 = ((bf16[8,8,3584]{2,1,0:T(8,128)(2,1)}), bf16[8,8,3584]{2,1,0:T(8,128)(2,1)S(1)}, u32[]{:S(2)}, u32[]{:S(2)}) async-start(bf16[8,8,3584]{2,1,0:T(8,128)(2,1)} %fusion.4), calls=%async_computation.5 | async-start | bytes 917504 | tf_op jit(solution)/shard_map/all_to_all | solution.py:73
  285.3 8.0 %collective-permute-start.19 = (bf16[64,3584]{1,0:T(8,128)(2,1)S(1)}, bf16[64,3584]{1,0:T(8,128)(2,1)S(1)}, u32[]{:S(2)}, u32[]{:S(2)}) collective-permute-start(bf16[64,3584]{1,0:T(8,128)(2,1)S(1)} %add_convert_fusion.3), channel_id=1, source_target_pairs={{0,32},{32,64},{64,96},{96,128},{128,160},{160,192},{192,224},{224... | collective-permute-start | bytes 1376264 | tf_op jit(solution)/shard_map/ppermute | solution.py:18
  295.2 13.0 %all-to-all-done.5 = bf16[8,8,3584]{2,1,0:T(8,128)(2,1)S(1)} async-done(((bf16[8,8,3584]{2,1,0:T(8,128)(2,1)}), bf16[8,8,3584]{2,1,0:T(8,128)(2,1)S(1)}, u32[]{:S(2)}, u32[]{:S(2)}) %all-to-all-start.5) | async-done | bytes 458784 | tf_op jit(solution)/shard_map/all_to_all | solution.py:73
  308.7 8.1 %collective-permute-start.20 = (bf16[16,3584]{1,0:T(8,128)(2,1)S(1)}, bf16[16,3584]{1,0:T(8,128)(2,1)S(1)}, u32[]{:S(2)}, u32[]{:S(2)}) collective-permute-start(bf16[16,3584]{1,0:T(8,128)(2,1)S(1)} %fusion.15), channel_id=1, source_target_pairs={{0,32},{32,64},{64,96},{96,128},{128,160},{160,192},{192,224},{224... | collective-permute-start | bytes 344072 | tf_op jit(solution)/shard_map/ppermute | solution.py:18
  320.2 7.0 %collective-permute-done.22 = bf16[16,3584]{1,0:T(8,128)(2,1)S(1)} collective-permute-done((bf16[16,3584]{1,0:T(8,128)(2,1)S(1)}, bf16[16,3584]{1,0:T(8,128)(2,1)S(1)}, u32[]{:S(2)}, u32[]{:S(2)}) %collective-permute-start.22) | collective-permute-done | bytes 114720 | tf_op jit(solution)/shard_map/ppermute | solution.py:18
  (131 shorter events, 65.6 us)
Async XLA Ops:
  0.6 32.2 %collective-permute-start.6 = (bf16[3584,128]{1,0:T(8,128)(2,1)}, bf16[3584,128]{1,0:T(8,128)(2,1)}, u32[]{:S(2)}, u32[]{:S(2)}) collective-permute-start(bf16[3584,128]{1,0:T(8,128)(2,1)} %bitcast.318), channel_id=1, source_target_pairs={{0,2},{2,0},{1,3},{3,1},{4,6},{6,4},{5,7},{7,5},{8,10},{10,8},{9,1... | collective-permute-start | bytes 2752520 | tf_op jit(solution)/shard_map/ppermute | solution.py:18
  4.5 33.2 %collective-permute-start.5 = (bf16[3584,128]{1,0:T(8,128)(2,1)}, bf16[3584,128]{1,0:T(8,128)(2,1)}, u32[]{:S(2)}, u32[]{:S(2)}) collective-permute-start(bf16[3584,128]{1,0:T(8,128)(2,1)} %bitcast.319), channel_id=1, source_target_pairs={{0,1},{1,0},{2,3},{3,2},{4,5},{5,4},{6,7},{7,6},{8,9},{9,8},{10,11... | collective-permute-start | bytes 2752520 | tf_op jit(solution)/shard_map/ppermute | solution.py:18
  8.6 26.6 %collective-permute-start = (bf16[3,64,16]{1,2,0:T(8,128)(2,1)S(1)}, bf16[3,64,16]{1,2,0:T(8,128)(2,1)S(1)}, u32[]{:S(2)}, u32[]{:S(2)}) collective-permute-start(bf16[3,64,16]{1,2,0:T(8,128)(2,1)S(1)} %bitcast.315), channel_id=1, source_target_pairs={{0,32},{32,64},{64,96},{96,128},{128,160},{160,192},{192,224},{224... | collective-permute-start | bytes 18440 | tf_op jit(solution)/shard_map/ppermute | solution.py:18
  12.8 76.9 %all-to-all-start = ((bf16[8,8,3584]{2,1,0:T(8,128)(2,1)}), bf16[8,8,3584]{2,1,0:T(8,128)(2,1)S(1)}, u32[]{:S(2)}, u32[]{:S(2)}) async-start(bf16[8,8,3584]{2,1,0:T(8,128)(2,1)} %bitcast.24), calls=%async_computation | async-start | bytes 917504 | tf_op jit(solution)/shard_map/all_to_all | solution.py:73
  26.6 42.3 %collective-permute-start.9 = (bf16[128,3584]{1,0:T(8,128)(2,1)}, bf16[128,3584]{1,0:T(8,128)(2,1)}, u32[]{:S(2)}, u32[]{:S(2)}) collective-permute-start(bf16[128,3584]{1,0:T(8,128)(2,1)} %bitcast.323), channel_id=1, source_target_pairs={{0,2},{2,0},{1,3},{3,1},{4,6},{6,4},{5,7},{7,5},{8,10},{10,8},{9,1... | collective-permute-start | bytes 2752520 | tf_op jit(solution)/shard_map/ppermute | solution.py:18
  29.5 58.1 %collective-permute-start.3 = (bf16[3584,128]{1,0:T(8,128)(2,1)}, bf16[3584,128]{1,0:T(8,128)(2,1)}, u32[]{:S(2)}, u32[]{:S(2)}) collective-permute-start(bf16[3584,128]{1,0:T(8,128)(2,1)} %bitcast.328), channel_id=1, source_target_pairs={{0,2},{2,0},{1,3},{3,1},{4,6},{6,4},{5,7},{7,5},{8,10},{10,8},{9,1... | collective-permute-start | bytes 2752520 | tf_op jit(solution)/shard_map/ppermute | solution.py:18
  32.8 56.8 %collective-permute-start.7 = (bf16[3584,128]{1,0:T(8,128)(2,1)}, bf16[3584,128]{1,0:T(8,128)(2,1)}, u32[]{:S(2)}, u32[]{:S(2)}) collective-permute-start(bf16[3584,128]{1,0:T(8,128)(2,1)} %collective-permute-done.6), channel_id=1, source_target_pairs={{0,1},{1,0},{2,3},{3,2},{4,5},{5,4},{6,7},{7,6},{8,9},{9,8},{10,11... | collective-permute-start | bytes 2752520 | tf_op jit(solution)/shard_map/ppermute | solution.py:18
  35.2 60.2 %collective-permute-start.8 = (bf16[128,3584]{1,0:T(8,128)(2,1)}, bf16[128,3584]{1,0:T(8,128)(2,1)}, u32[]{:S(2)}, u32[]{:S(2)}) collective-permute-start(bf16[128,3584]{1,0:T(8,128)(2,1)} %bitcast.324), channel_id=1, source_target_pairs={{0,1},{1,0},{2,3},{3,2},{4,5},{5,4},{6,7},{7,6},{8,9},{9,8},{10,11... | collective-permute-start | bytes 2752520 | tf_op jit(solution)/shard_map/ppermute | solution.py:18
  37.6 60.3 %collective-permute-start.2 = (bf16[3584,128]{1,0:T(8,128)(2,1)}, bf16[3584,128]{1,0:T(8,128)(2,1)}, u32[]{:S(2)}, u32[]{:S(2)}) collective-permute-start(bf16[3584,128]{1,0:T(8,128)(2,1)} %bitcast.329), channel_id=1, source_target_pairs={{0,1},{1,0},{2,3},{3,2},{4,5},{5,4},{6,7},{7,6},{8,9},{9,8},{10,11... | collective-permute-start | bytes 2752520 | tf_op jit(solution)/shard_map/ppermute | solution.py:18
  68.9 32.8 %collective-permute-start.10 = (bf16[128,3584]{1,0:T(8,128)(2,1)}, bf16[128,3584]{1,0:T(8,128)(2,1)}, u32[]{:S(2)}, u32[]{:S(2)}) collective-permute-start(bf16[128,3584]{1,0:T(8,128)(2,1)} %collective-permute-done.9), channel_id=1, source_target_pairs={{0,1},{1,0},{2,3},{3,2},{4,5},{5,4},{6,7},{7,6},{8,9},{9,8},{10,11... | collective-permute-start | bytes 2752520 | tf_op jit(solution)/shard_map/ppermute | solution.py:18
  87.7 14.0 %collective-permute-start.4 = (bf16[3584,128]{1,0:T(8,128)(2,1)}, bf16[3584,128]{1,0:T(8,128)(2,1)}, u32[]{:S(2)}, u32[]{:S(2)}) collective-permute-start(bf16[3584,128]{1,0:T(8,128)(2,1)} %collective-permute-done.3), channel_id=1, source_target_pairs={{0,1},{1,0},{2,3},{3,2},{4,5},{5,4},{6,7},{7,6},{8,9},{9,8},{10,11... | collective-permute-start | bytes 2752520 | tf_op jit(solution)/shard_map/ppermute | solution.py:18
  89.6 69.9 %collective-permute-start.1 = (bf16[64,3584]{1,0:T(8,128)(2,1)S(1)}, bf16[64,3584]{1,0:T(8,128)(2,1)S(1)}, u32[]{:S(2)}, u32[]{:S(2)}) collective-permute-start(bf16[64,3584]{1,0:T(8,128)(2,1)S(1)} %bitcast.289), channel_id=1, source_target_pairs={{0,32},{32,64},{64,96},{96,128},{128,160},{160,192},{192,224},{224... | collective-permute-start | bytes 1376264 | tf_op jit(solution)/shard_map/ppermute | solution.py:18
  95.4 23.0 %collective-permute-start.12 = (bf16[3,64,16]{1,2,0:T(8,128)(2,1)S(1)}, bf16[3,64,16]{1,2,0:T(8,128)(2,1)S(1)}, u32[]{:S(2)}, u32[]{:S(2)}) collective-permute-start(bf16[3,64,16]{1,2,0:T(8,128)(2,1)S(1)} %bitcast.314), channel_id=1, source_target_pairs={{0,480},{32,0},{64,32},{96,64},{128,96},{160,128},{192,160},{224,1... | collective-permute-start | bytes 18440 | tf_op jit(solution)/shard_map/ppermute | solution.py:18
  98.0 61.3 %collective-permute-start.13 = (bf16[64,3584]{1,0:T(8,128)(2,1)S(1)}, bf16[64,3584]{1,0:T(8,128)(2,1)S(1)}, u32[]{:S(2)}, u32[]{:S(2)}) collective-permute-start(bf16[64,3584]{1,0:T(8,128)(2,1)S(1)} %bitcast.290), channel_id=1, source_target_pairs={{0,480},{32,0},{64,32},{96,64},{128,96},{160,128},{192,160},{224,1... | collective-permute-start | bytes 1376264 | tf_op jit(solution)/shard_map/ppermute | solution.py:18
  107.0 39.7 %all-to-all-start.1 = ((bf16[8,8,3584]{2,1,0:T(8,128)(2,1)}), bf16[8,8,3584]{2,1,0:T(8,128)(2,1)S(1)}, u32[]{:S(2)}, u32[]{:S(2)}) async-start(bf16[8,8,3584]{2,1,0:T(8,128)(2,1)} %fusion.2), calls=%async_computation.1 | async-start | bytes 917504 | tf_op jit(solution)/shard_map/all_to_all | solution.py:73
  160.8 30.6 %all-to-all-start.2 = ((bf16[8,8,3584]{2,1,0:T(8,128)(2,1)}), bf16[8,8,3584]{2,1,0:T(8,128)(2,1)S(1)}, u32[]{:S(2)}, u32[]{:S(2)}) async-start(bf16[8,8,3584]{2,1,0:T(8,128)(2,1)} %bitcast.49), calls=%async_computation.2 | async-start | bytes 917504 | tf_op jit(solution)/shard_map/all_to_all | solution.py:73
  198.9 22.3 %all-to-all-start.3 = ((bf16[8,8,3584]{2,1,0:T(8,128)(2,1)}), bf16[8,8,3584]{2,1,0:T(8,128)(2,1)S(1)}, u32[]{:S(2)}, u32[]{:S(2)}) async-start(bf16[8,8,3584]{2,1,0:T(8,128)(2,1)} %fusion.3), calls=%async_computation.3 | async-start | bytes 917504 | tf_op jit(solution)/shard_map/all_to_all | solution.py:73
  204.0 32.6 %collective-permute-start.15 = (bf16[64,3584]{1,0:T(8,128)(2,1)S(1)}, bf16[64,3584]{1,0:T(8,128)(2,1)S(1)}, u32[]{:S(2)}, u32[]{:S(2)}) collective-permute-start(bf16[64,3584]{1,0:T(8,128)(2,1)S(1)} %add_convert_fusion.5), channel_id=1, source_target_pairs={{0,32},{32,64},{64,96},{96,128},{128,160},{160,192},{192,224},{224... | collective-permute-start | bytes 1376264 | tf_op jit(solution)/shard_map/ppermute | solution.py:18
  211.3 25.1 %collective-permute-start.17 = (bf16[64,3584]{1,0:T(8,128)(2,1)S(1)}, bf16[64,3584]{1,0:T(8,128)(2,1)S(1)}, u32[]{:S(2)}, u32[]{:S(2)}) collective-permute-start(bf16[64,3584]{1,0:T(8,128)(2,1)S(1)} %add_convert_fusion.4), channel_id=1, source_target_pairs={{0,480},{32,0},{64,32},{96,64},{128,96},{160,128},{192,160},{224,1... | collective-permute-start | bytes 1376264 | tf_op jit(solution)/shard_map/ppermute | solution.py:18
  221.7 12.5 %collective-permute-start.18 = (bf16[16,3584]{1,0:T(8,128)(2,1)S(1)}, bf16[16,3584]{1,0:T(8,128)(2,1)S(1)}, u32[]{:S(2)}, u32[]{:S(2)}) collective-permute-start(bf16[16,3584]{1,0:T(8,128)(2,1)S(1)} %fusion.14), channel_id=1, source_target_pairs={{0,480},{32,0},{64,32},{96,64},{128,96},{160,128},{192,160},{224,1... | collective-permute-start | bytes 344072 | tf_op jit(solution)/shard_map/ppermute | solution.py:18
  237.9 35.3 %all-to-all-start.4 = ((bf16[8,8,3584]{2,1,0:T(8,128)(2,1)}), bf16[8,8,3584]{2,1,0:T(8,128)(2,1)S(1)}, u32[]{:S(2)}, u32[]{:S(2)}) async-start(bf16[8,8,3584]{2,1,0:T(8,128)(2,1)} %bitcast.75), calls=%async_computation.4 | async-start | bytes 917504 | tf_op jit(solution)/shard_map/all_to_all | solution.py:73
  280.9 27.3 %all-to-all-start.5 = ((bf16[8,8,3584]{2,1,0:T(8,128)(2,1)}), bf16[8,8,3584]{2,1,0:T(8,128)(2,1)S(1)}, u32[]{:S(2)}, u32[]{:S(2)}) async-start(bf16[8,8,3584]{2,1,0:T(8,128)(2,1)} %fusion.4), calls=%async_computation.5 | async-start | bytes 917504 | tf_op jit(solution)/shard_map/all_to_all | solution.py:73
  285.3 33.9 %collective-permute-start.19 = (bf16[64,3584]{1,0:T(8,128)(2,1)S(1)}, bf16[64,3584]{1,0:T(8,128)(2,1)S(1)}, u32[]{:S(2)}, u32[]{:S(2)}) collective-permute-start(bf16[64,3584]{1,0:T(8,128)(2,1)S(1)} %add_convert_fusion.3), channel_id=1, source_target_pairs={{0,32},{32,64},{64,96},{96,128},{128,160},{160,192},{192,224},{224... | collective-permute-start | bytes 1376264 | tf_op jit(solution)/shard_map/ppermute | solution.py:18
  293.3 26.9 %collective-permute-start.21 = (bf16[64,3584]{1,0:T(8,128)(2,1)S(1)}, bf16[64,3584]{1,0:T(8,128)(2,1)S(1)}, u32[]{:S(2)}, u32[]{:S(2)}) collective-permute-start(bf16[64,3584]{1,0:T(8,128)(2,1)S(1)} %add_convert_fusion.2), channel_id=1, source_target_pairs={{0,480},{32,0},{64,32},{96,64},{128,96},{160,128},{192,160},{224,1... | collective-permute-start | bytes 1376264 | tf_op jit(solution)/shard_map/ppermute | solution.py:18
  (9 other events, 84.0 us)
